TPU v7x, 256 devices: a whole 4x4x8 slice. The times are simulated.
256 devices in a mesh: grp: 8 (over x, y_hi), blk: 32 (over z, y_lo, core).
Axes of the slice: x: 4, y: 4 (y_hi: 2, y_lo: 2; y = y_hi * 2 + y_lo), z: 8, core: 2. Of those that a mesh axis runs over, the one named last changes fastest.
Arguments:
- counts: int32 [65536, 1024], P(('grp', 'blk')), may hold values from 0 to 5
- tile_live: int32 [512, 8], P(('grp', 'blk')), may hold values from 0 to 1
- doc_lengths: int32 [65536], P(('grp', 'blk')), may hold values from 256 to 4095
- doc_mix: bfloat16 [65536, 4096], P(('grp', 'blk')), may hold values from 0.019897461 to 50
- word_topic: float32 [4096, 4096], P('blk'), may hold values from 0.01 to 8
- topic_total: float32 [4096], replicated, may hold values from 20000 to 400000
Outputs:
- doc_share: bfloat16 [65536, 4096], P(('grp', 'blk'))
- word_topic_new: float32 [4096, 4096], P('blk')
- topic_mean: float32 [4096], replicated
All inputs are finite; a program needn't handle non-finite values.
Results may differ from a plain program's by a relative error of at most 0.0004.
The roundings to bfloat16 on the way count: a program that leaves them out, or rounds other values in their place, can miss the bound.
Values may be sent and summed in bfloat16 or wider, within the bound.
A program may use at most 128 MiB of HBM per device.

v0:
```python
import jax
import jax.numpy as jnp
from jax import lax
from jax.sharding import PartitionSpec as P

VOCAB = 262144
alpha_prior = 0.1
beta_prior = 0.01


def passed_along(block, axis, distance):
    devices = range(lax.axis_size(axis))
    route = [((i - distance) % len(devices), i) for i in devices]
    return lax.ppermute(block, axis, route)


def tile_terms(operands):
    doc_rows, block_counts, visitor = operands
    normalizer = jnp.dot(doc_rows, visitor.T, preferred_element_type=jnp.float32)
    ratio = (block_counts / normalizer).astype(jnp.bfloat16)
    doc_part = jnp.dot(ratio, visitor, preferred_element_type=jnp.float32)
    word_part = jnp.dot(ratio.T, doc_rows, preferred_element_type=jnp.float32)
    return (doc_part, word_part)


def shard_terms(visitor, block_counts, doc_low):
    return tile_terms((doc_low, block_counts, visitor))


def local(counts, tile_live, doc_lengths, doc_mix, word_topic, topic_total):
    block_rows = word_topic.shape[0]
    visits = tile_live.shape[1]
    word_weight = (word_topic + beta_prior) / (topic_total + beta_prior * VOCAB)[None, :]
    word_low = word_weight.astype(jnp.bfloat16)
    mix_wide = doc_mix.astype(jnp.float32)
    doc_theta = mix_wide / jnp.sum(mix_wide, axis=1, keepdims=True)
    doc_weight = doc_lengths.astype(jnp.float32)[:, None] * doc_theta + alpha_prior
    doc_low = doc_weight.astype(jnp.bfloat16)
    live_full = jnp.repeat(jnp.repeat(tile_live, block_rows, axis=0), block_rows, axis=1)
    live_counts = counts.astype(jnp.float32) * live_full.astype(jnp.float32)
    window_len = jnp.sum(live_counts, axis=1)
    doc_proj = jnp.zeros((doc_low.shape[0], doc_low.shape[1]), jnp.float32)
    word_accum = jnp.zeros((block_rows, doc_low.shape[1]), jnp.float32)
    visitor = word_low
    for offset in range(visits):
        if offset > 0:
            visitor, word_accum = (
                passed_along(visitor.astype(jnp.float32), "blk", -1).astype(visitor.dtype),
                passed_along(word_accum, "blk", -1),
            )
        block_counts = live_counts[:, offset * block_rows : (offset + 1) * block_rows]
        doc_part, word_part = shard_terms(visitor, block_counts, doc_low)
        doc_proj = doc_proj + doc_part
        word_accum = word_accum + word_part
    word_accum = passed_along(word_accum, "blk", visits - 1)
    doc_new = doc_weight * doc_proj
    column_sum = jnp.sum(doc_new, axis=0)
    topic_count = doc_low.shape[1]
    doc_share = (
        topic_count * (doc_new + alpha_prior) / (window_len[:, None] + topic_count * alpha_prior)
    ).astype(jnp.bfloat16)
    word_sum = lax.psum(word_accum, "grp")
    topic_sum = lax.psum(column_sum, ("grp", "blk"))
    vocab_window = block_rows * lax.axis_size("blk")
    return (doc_share, word_weight * word_sum, topic_sum / vocab_window)


def solution(mesh):
    return jax.shard_map(
        local,
        mesh=mesh,
        in_specs=(
            P(("grp", "blk"), None),
            P(("grp", "blk"), None),
            P(("grp", "blk")),
            P(("grp", "blk"), None),
            P("blk", None),
            P(),
        ),
        out_specs=(P(("grp", "blk"), None), P("blk", None), P()),
        check_vma=False,
    )
```

profile of v0, /device:TPU:161, one launch (start us, length us, event | category | flops | bytes accessed | tf_op | source)
XLA Modules:
  0.0 519.2 jit_solution(7656554678656352072)
XLA Ops:
  7.2 0.8 convert_element_type.95
  8.1 2.0 convert_reduce_fusion
  10.0 0.7 broadcast_add_fusion
  10.7 1.0 fusion.8
  12.4 1.0 copy-done
  13.7 0.7 fusion.9
  14.8 0.8 collective-permute-start.7
  15.6 1.5 collective-permute-start
  17.1 34.7 %collective-permute-done = bf16[128,4096]{1,0:T(8,128)(2,1)S(1)} collective-permute-done((bf16[128,4096]{1,0:T(8,128)(2,1)S(1)}, bf16[128,4096]{1,0:T(8,128)(2,1)S(1)}, u32[]{:S(2)}, u32[]{:S(2)}) %collective-permute-start) | collective-permute-done | bytes 1048608 | tf_op jit(solution)/shard_map/ppermute | solution.py:14
  51.7 0.7 fusion.10
  52.5 0.5 convolution_add_fusion.2
  53.2 2.8 collective-permute-start.1
  56.0 33.8 %collective-permute-done.1 = bf16[128,4096]{1,0:T(8,128)(2,1)S(1)} collective-permute-done((bf16[128,4096]{1,0:T(8,128)(2,1)S(1)}, bf16[128,4096]{1,0:T(8,128)(2,1)S(1)}, u32[]{:S(2)}, u32[]{:S(2)}) %collective-permute-start.1) | collective-permute-done | bytes 1048608 | tf_op jit(solution)/shard_map/ppermute | solution.py:14
  89.8 0.7 fusion.11
  90.5 0.5 fusion.42
  91.3 1.1 collective-permute-start.9
  92.4 2.8 collective-permute-start.2
  95.2 32.9 %collective-permute-done.2 = bf16[128,4096]{1,0:T(8,128)(2,1)S(1)} collective-permute-done((bf16[128,4096]{1,0:T(8,128)(2,1)S(1)}, bf16[128,4096]{1,0:T(8,128)(2,1)S(1)}, u32[]{:S(2)}, u32[]{:S(2)}) %collective-permute-start.2) | collective-permute-done | bytes 1048608 | tf_op jit(solution)/shard_map/ppermute | solution.py:14
  128.0 0.7 fusion.12
  129.5 2.0 collective-permute-start.10
  131.5 2.8 collective-permute-start.3
  134.3 32.0 %collective-permute-done.3 = bf16[128,4096]{1,0:T(8,128)(2,1)S(1)} collective-permute-done((bf16[128,4096]{1,0:T(8,128)(2,1)S(1)}, bf16[128,4096]{1,0:T(8,128)(2,1)S(1)}, u32[]{:S(2)}, u32[]{:S(2)}) %collective-permute-start.3) | collective-permute-done | bytes 1048608 | tf_op jit(solution)/shard_map/ppermute | solution.py:14
  166.3 0.7 fusion.13
  167.7 2.9 collective-permute-start.11
  170.6 2.8 collective-permute-start.4
  173.4 31.1 %collective-permute-done.4 = bf16[128,4096]{1,0:T(8,128)(2,1)S(1)} collective-permute-done((bf16[128,4096]{1,0:T(8,128)(2,1)S(1)}, bf16[128,4096]{1,0:T(8,128)(2,1)S(1)}, u32[]{:S(2)}, u32[]{:S(2)}) %collective-permute-start.4) | collective-permute-done | bytes 1048608 | tf_op jit(solution)/shard_map/ppermute | solution.py:14
  204.5 0.7 fusion.14
  206.0 3.8 collective-permute-start.12
  209.8 2.8 collective-permute-start.5
  212.6 30.2 %collective-permute-done.5 = bf16[128,4096]{1,0:T(8,128)(2,1)S(1)} collective-permute-done((bf16[128,4096]{1,0:T(8,128)(2,1)S(1)}, bf16[128,4096]{1,0:T(8,128)(2,1)S(1)}, u32[]{:S(2)}, u32[]{:S(2)}) %collective-permute-start.5) | collective-permute-done | bytes 1048608 | tf_op jit(solution)/shard_map/ppermute | solution.py:14
  242.7 0.7 fusion.15
  244.2 4.7 collective-permute-start.13
  248.9 2.8 collective-permute-start.6
  251.7 0.7 fusion.40
  252.4 28.6 %collective-permute-done.6 = bf16[128,4096]{1,0:T(8,128)(2,1)S(1)} collective-permute-done((bf16[128,4096]{1,0:T(8,128)(2,1)S(1)}, bf16[128,4096]{1,0:T(8,128)(2,1)S(1)}, u32[]{:S(2)}, u32[]{:S(2)}) %collective-permute-start.6) | collective-permute-done | bytes 1048608 | tf_op jit(solution)/shard_map/ppermute | solution.py:14
  281.0 0.7 fusion.16
  282.4 6.9 %collective-permute-start.14 = (f32[128,4096]{1,0:T(8,128)S(1)}, f32[128,4096]{1,0:T(8,128)}, u32[]{:S(2)}, u32[]{:S(2)}) collective-permute-start(f32[128,4096]{1,0:T(8,128)S(1)} %add.96), channel_id=1, source_target_pairs={{25,0},{26,1},{27,2},{28,3},{29,4},{30,5},{31,6},{0,7},{1,8},{2,9}... | collective-permute-start | bytes 6291464 | tf_op jit(solution)/shard_map/ppermute | solution.py:14
  289.3 2.7 convolution_add_fusion.1
  292.0 2.6 fusion.52
  294.6 2.6 fusion.51
  297.2 2.7 fusion.50
  299.9 2.7 fusion.49
  302.6 2.6 fusion.48
  305.2 69.0 %collective-permute-done.14 = f32[128,4096]{1,0:T(8,128)} collective-permute-done((f32[128,4096]{1,0:T(8,128)S(1)}, f32[128,4096]{1,0:T(8,128)}, u32[]{:S(2)}, u32[]{:S(2)}) %collective-permute-start.14) | collective-permute-done | bytes 2097184 | tf_op jit(solution)/shard_map/ppermute | solution.py:14
  374.2 11.5 %fusion.39 = (f32[4096]{0:T(1024)S(1)}, bf16[256,4096]{1,0:T(8,128)(2,1)}) fusion(f32[256]{0:T(256)S(1)} %broadcast_add_fusion.1, f32[256,4096]{1,0:T(8,128)} %fusion.48, f32[256,4096]{1,0:T(8,128)} %fusion.49, f32[256,4096]{1,0:T(8,128)} %fusion.50, f32[256,4096]{1,0:T(8,128)} %fusion.51, f32[256,4096]{1,0:T(8,128)} %fusion.52, ...), kind=kOutput, calls=%fused_computation.64 | convolution fusion | flops 285208576 | bytes 30493696 | tf_op jit(solution)/shard_map/dot_general | solution.py:21
  385.7 122.8 %psum.15 = f32[4096]{0:T(1024)S(1)} all-reduce(f32[4096]{0:T(1024)S(1)} %get-tuple-element.5), channel_id=1, replica_groups=mesh['grp'=8,'blk'=32] {'grp','blk'}, use_global_device_ids=true, to_apply=%region_4.0 | all-reduce | flops 4096 | bytes 32768 | tf_op jit(solution)/shard_map/psum | solution.py:63
  508.5 0.6 broadcast_multiply_fusion
  509.1 3.2 fusion.17
  (36 shorter events, 5.5 us)
Async XLA Ops:
  7.2 3.6 copy-start.1
  7.2 2.8 copy-start.3
  7.2 501.9 %all-reduce.2.cloned.1.call-start = ((), (), s32[]{:S(2)}) async-start(), calls=%async_computation | async-start | bytes 4194304 | tf_op jit(solution)/shard_map/psum | solution.py:62
  10.7 1.4 copy-start.2
  11.8 1.6 copy-start
  14.8 37.6 %collective-permute-start.7 = (f32[128,4096]{1,0:T(8,128)S(1)}, f32[128,4096]{1,0:T(8,128)S(1)}, u32[]{:S(2)}, u32[]{:S(2)}) collective-permute-start(f32[128,4096]{1,0:T(8,128)S(1)} %fusion.41), channel_id=1, source_target_pairs={{1,0},{2,1},{3,2},{4,3},{5,4},{6,5},{7,6},{8,7},{9,8},{10,9},{11,1... | collective-permute-start | bytes 6291464 | tf_op jit(solution)/shard_map/ppermute | solution.py:14
  15.6 36.1 %collective-permute-start = (bf16[128,4096]{1,0:T(8,128)(2,1)S(1)}, bf16[128,4096]{1,0:T(8,128)(2,1)S(1)}, u32[]{:S(2)}, u32[]{:S(2)}) collective-permute-start(bf16[128,4096]{1,0:T(8,128)(2,1)S(1)} %fusion.18), channel_id=1, source_target_pairs={{1,0},{2,1},{3,2},{4,3},{5,4},{6,5},{7,6},{8,7},{9,8},{10,9},{11,1... | collective-permute-start | bytes 3145736 | tf_op jit(solution)/shard_map/ppermute | solution.py:14
  53.0 38.0 %collective-permute-start.8 = (f32[128,4096]{1,0:T(8,128)S(1)}, f32[128,4096]{1,0:T(8,128)S(1)}, u32[]{:S(2)}, u32[]{:S(2)}) collective-permute-start(f32[128,4096]{1,0:T(8,128)S(1)} %convolution_add_fusion.2), channel_id=1, source_target_pairs={{1,0},{2,1},{3,2},{4,3},{5,4},{6,5},{7,6},{8,7},{9,8},{10,9},{11,1... | collective-permute-start | bytes 6291464 | tf_op jit(solution)/shard_map/ppermute | solution.py:14
  53.2 36.6 %collective-permute-start.1 = (bf16[128,4096]{1,0:T(8,128)(2,1)S(1)}, bf16[128,4096]{1,0:T(8,128)(2,1)S(1)}, u32[]{:S(2)}, u32[]{:S(2)}) collective-permute-start(bf16[128,4096]{1,0:T(8,128)(2,1)S(1)} %collective-permute-done), channel_id=1, source_target_pairs={{1,0},{2,1},{3,2},{4,3},{5,4},{6,5},{7,6},{8,7},{9,8},{10,9},{11,1... | collective-permute-start | bytes 3145736 | tf_op jit(solution)/shard_map/ppermute | solution.py:14
  91.3 38.0 %collective-permute-start.9 = (f32[128,4096]{1,0:T(8,128)S(1)}, f32[128,4096]{1,0:T(8,128)S(1)}, u32[]{:S(2)}, u32[]{:S(2)}) collective-permute-start(f32[128,4096]{1,0:T(8,128)S(1)} %add.91), channel_id=1, source_target_pairs={{1,0},{2,1},{3,2},{4,3},{5,4},{6,5},{7,6},{8,7},{9,8},{10,9},{11,1... | collective-permute-start | bytes 6291464 | tf_op jit(solution)/shard_map/ppermute | solution.py:14
  92.4 35.7 %collective-permute-start.2 = (bf16[128,4096]{1,0:T(8,128)(2,1)S(1)}, bf16[128,4096]{1,0:T(8,128)(2,1)S(1)}, u32[]{:S(2)}, u32[]{:S(2)}) collective-permute-start(bf16[128,4096]{1,0:T(8,128)(2,1)S(1)} %collective-permute-done.1), channel_id=1, source_target_pairs={{1,0},{2,1},{3,2},{4,3},{5,4},{6,5},{7,6},{8,7},{9,8},{10,9},{11,1... | collective-permute-start | bytes 3145736 | tf_op jit(solution)/shard_map/ppermute | solution.py:14
  129.5 38.0 %collective-permute-start.10 = (f32[128,4096]{1,0:T(8,128)S(1)}, f32[128,4096]{1,0:T(8,128)S(1)}, u32[]{:S(2)}, u32[]{:S(2)}) collective-permute-start(f32[128,4096]{1,0:T(8,128)S(1)} %add.92), channel_id=1, source_target_pairs={{1,0},{2,1},{3,2},{4,3},{5,4},{6,5},{7,6},{8,7},{9,8},{10,9},{11,1... | collective-permute-start | bytes 6291464 | tf_op jit(solution)/shard_map/ppermute | solution.py:14
  131.5 34.8 %collective-permute-start.3 = (bf16[128,4096]{1,0:T(8,128)(2,1)S(1)}, bf16[128,4096]{1,0:T(8,128)(2,1)S(1)}, u32[]{:S(2)}, u32[]{:S(2)}) collective-permute-start(bf16[128,4096]{1,0:T(8,128)(2,1)S(1)} %collective-permute-done.2), channel_id=1, source_target_pairs={{1,0},{2,1},{3,2},{4,3},{5,4},{6,5},{7,6},{8,7},{9,8},{10,9},{11,1... | collective-permute-start | bytes 3145736 | tf_op jit(solution)/shard_map/ppermute | solution.py:14
  167.7 38.0 %collective-permute-start.11 = (f32[128,4096]{1,0:T(8,128)S(1)}, f32[128,4096]{1,0:T(8,128)S(1)}, u32[]{:S(2)}, u32[]{:S(2)}) collective-permute-start(f32[128,4096]{1,0:T(8,128)S(1)} %add.93), channel_id=1, source_target_pairs={{1,0},{2,1},{3,2},{4,3},{5,4},{6,5},{7,6},{8,7},{9,8},{10,9},{11,1... | collective-permute-start | bytes 6291464 | tf_op jit(solution)/shard_map/ppermute | solution.py:14
  170.6 33.9 %collective-permute-start.4 = (bf16[128,4096]{1,0:T(8,128)(2,1)S(1)}, bf16[128,4096]{1,0:T(8,128)(2,1)S(1)}, u32[]{:S(2)}, u32[]{:S(2)}) collective-permute-start(bf16[128,4096]{1,0:T(8,128)(2,1)S(1)} %collective-permute-done.3), channel_id=1, source_target_pairs={{1,0},{2,1},{3,2},{4,3},{5,4},{6,5},{7,6},{8,7},{9,8},{10,9},{11,1... | collective-permute-start | bytes 3145736 | tf_op jit(solution)/shard_map/ppermute | solution.py:14
  206.0 38.0 %collective-permute-start.12 = (f32[128,4096]{1,0:T(8,128)S(1)}, f32[128,4096]{1,0:T(8,128)S(1)}, u32[]{:S(2)}, u32[]{:S(2)}) collective-permute-start(f32[128,4096]{1,0:T(8,128)S(1)} %add.94), channel_id=1, source_target_pairs={{1,0},{2,1},{3,2},{4,3},{5,4},{6,5},{7,6},{8,7},{9,8},{10,9},{11,1... | collective-permute-start | bytes 6291464 | tf_op jit(solution)/shard_map/ppermute | solution.py:14
  209.8 33.0 %collective-permute-start.5 = (bf16[128,4096]{1,0:T(8,128)(2,1)S(1)}, bf16[128,4096]{1,0:T(8,128)(2,1)S(1)}, u32[]{:S(2)}, u32[]{:S(2)}) collective-permute-start(bf16[128,4096]{1,0:T(8,128)(2,1)S(1)} %collective-permute-done.4), channel_id=1, source_target_pairs={{1,0},{2,1},{3,2},{4,3},{5,4},{6,5},{7,6},{8,7},{9,8},{10,9},{11,1... | collective-permute-start | bytes 3145736 | tf_op jit(solution)/shard_map/ppermute | solution.py:14
  244.2 38.0 %collective-permute-start.13 = (f32[128,4096]{1,0:T(8,128)S(1)}, f32[128,4096]{1,0:T(8,128)S(1)}, u32[]{:S(2)}, u32[]{:S(2)}) collective-permute-start(f32[128,4096]{1,0:T(8,128)S(1)} %add.95), channel_id=1, source_target_pairs={{1,0},{2,1},{3,2},{4,3},{5,4},{6,5},{7,6},{8,7},{9,8},{10,9},{11,1... | collective-permute-start | bytes 6291464 | tf_op jit(solution)/shard_map/ppermute | solution.py:14
  248.9 32.1 %collective-permute-start.6 = (bf16[128,4096]{1,0:T(8,128)(2,1)S(1)}, bf16[128,4096]{1,0:T(8,128)(2,1)S(1)}, u32[]{:S(2)}, u32[]{:S(2)}) collective-permute-start(bf16[128,4096]{1,0:T(8,128)(2,1)S(1)} %collective-permute-done.5), channel_id=1, source_target_pairs={{1,0},{2,1},{3,2},{4,3},{5,4},{6,5},{7,6},{8,7},{9,8},{10,9},{11,1... | collective-permute-start | bytes 3145736 | tf_op jit(solution)/shard_map/ppermute | solution.py:14
  282.4 91.8 %collective-permute-start.14 = (f32[128,4096]{1,0:T(8,128)S(1)}, f32[128,4096]{1,0:T(8,128)}, u32[]{:S(2)}, u32[]{:S(2)}) collective-permute-start(f32[128,4096]{1,0:T(8,128)S(1)} %add.96), channel_id=1, source_target_pairs={{25,0},{26,1},{27,2},{28,3},{29,4},{30,5},{31,6},{0,7},{1,8},{2,9}... | collective-permute-start | bytes 6291464 | tf_op jit(solution)/shard_map/ppermute | solution.py:14
Sparse Core Ops, SparseCore 0:
  374.3 117.2 all-reduce.1
where the time goes:
time: 520 us; the launch traced here: 519 us
  waiting for transfers between devices  292 us (56%)
  blocking collectives  123 us (24%)
  starting transfers between devices  40.6 us (8%)
  matrix products  37.6 us (7%)
  between operations  14.3 us (3%)
  other arithmetic  10.4 us (2%)
    ppermute x15, waiting for transfers between devices, passed_along(): return lax.ppermute(block, axis, route)  292 us
    psum x1, blocking collectives, local(): topic_sum = lax.psum(column_sum, ('grp', 'blk'))  123 us
    ppermute x15, starting transfers between devices, passed_along(): return lax.ppermute(block, axis, route)  40.6 us
    dot_general x8, matrix products, tile_terms(): doc_part = jnp.dot(ratio, visitor, preferred_element_type=jnp.float32)  28.1 us
  transfers between devices with their start and end apart: 16, of which 8 were waited for; matrix products, arithmetic and copies ran while one was open for 7% of the time, Pallas kernels for 0%

commit v1 on v0

--- a/solution.py
+++ b/solution.py
@@ -60,7 +60,7 @@
         topic_count * (doc_new + alpha_prior) / (window_len[:, None] + topic_count * alpha_prior)
     ).astype(jnp.bfloat16)
     word_sum = lax.psum(word_accum, "grp")
-    topic_sum = lax.psum(column_sum, ("grp", "blk"))
+    topic_sum = jnp.sum(lax.all_gather(column_sum, ("grp", "blk")), axis=0)
     vocab_window = block_rows * lax.axis_size("blk")
     return (doc_share, word_weight * word_sum, topic_sum / vocab_window)
 

time: 520 us -> 769 us (1.48); the launches traced: 519 us -> 760 us
  waiting for transfers between devices: 292 us -> 663 us
  blocking collectives: 123 us -> 0 us
  matrix products: 37.6 us -> 27.9 us
  starting transfers between devices: 40.6 us -> 32.4 us
    all_gather x0 -> x1, waiting for transfers between devices: none -> 390 us  [local(): topic_sum = jnp.sum(lax.all_gather(column_sum, ('grp', 'blk')), axis=0)]
    psum x1 -> x0, blocking collectives: 123 us -> none  [local(): topic_sum = lax.psum(column_sum, ('grp', 'blk'))]
    ppermute x15, waiting for transfers between devices: 292 us -> 272 us  [passed_along(): return lax.ppermute(block, axis, route)]
    dot_general x8, matrix products: 28.1 us -> 17.4 us  [tile_terms(): doc_part = jnp.dot(ratio, visitor, preferred_element_type=jnp.float32)]
    ppermute x15, starting transfers between devices: 40.6 us -> 32.3 us  [passed_along(): return lax.ppermute(block, axis, route)]
  transfers between devices with their start and end apart: 16 -> 17, of which waited for: 8 -> 13; matrix products, arithmetic and copies ran while one was open for 7% -> 5% of each run, Pallas kernels for 0% -> 0%
where the time goes in v1:
time: 769 us; the launch traced here: 760 us
  waiting for transfers between devices  663 us (86%)
  starting transfers between devices  32.4 us (4%)
  matrix products  27.9 us (4%)
  between operations  15.8 us (2%)
  other arithmetic  15.3 us (2%)
    all_gather x1, waiting for transfers between devices, local(): topic_sum = jnp.sum(lax.all_gather(column_sum, ('grp', 'blk')), axis=0)  390 us
    ppermute x15, waiting for transfers between devices, passed_along(): return lax.ppermute(block, axis, route)  272 us
    ppermute x15, starting transfers between devices, passed_along(): return lax.ppermute(block, axis, route)  32.3 us
    dot_general x8, matrix products, tile_terms(): doc_part = jnp.dot(ratio, visitor, preferred_element_type=jnp.float32)  17.4 us
  transfers between devices with their start and end apart: 17, of which 13 were waited for; matrix products, arithmetic and copies ran while one was open for 5% of the time, Pallas kernels for 0%

profile of v1, /device:TPU:161, one launch (start us, length us, event | category | flops | bytes accessed | tf_op | source)
XLA Modules:
  0.0 760.1 jit_solution(70079653835055854)
XLA Ops:
  8.1 0.9 broadcast_add_fusion
  8.9 2.0 fusion.18
  10.9 0.8 collective-permute-start
  12.1 1.0 fusion.8
  13.7 0.7 fusion.9
  15.0 1.5 collective-permute-start.7
  16.5 8.9 %collective-permute-done = bf16[128,4096]{1,0:T(8,128)(2,1)S(1)} collective-permute-done((bf16[128,4096]{1,0:T(8,128)(2,1)S(1)}, bf16[128,4096]{1,0:T(8,128)(2,1)S(1)}, u32[]{:S(2)}, u32[]{:S(2)}) %collective-permute-start) | collective-permute-done | bytes 1048608 | tf_op jit(solution)/shard_map/ppermute | solution.py:14
  25.4 0.7 fusion.10
  26.2 32.9 %collective-permute-done.1 = bf16[128,4096]{1,0:T(8,128)(2,1)S(1)} collective-permute-done((bf16[128,4096]{1,0:T(8,128)(2,1)S(1)}, bf16[128,4096]{1,0:T(8,128)(2,1)S(1)}, u32[]{:S(2)}, u32[]{:S(2)}) %collective-permute-start.1) | collective-permute-done | bytes 1048608 | tf_op jit(solution)/shard_map/ppermute | solution.py:14
  59.7 2.9 collective-permute-start.8
  62.6 10.7 %collective-permute-done.2 = bf16[128,4096]{1,0:T(8,128)(2,1)S(1)} collective-permute-done((bf16[128,4096]{1,0:T(8,128)(2,1)S(1)}, bf16[128,4096]{1,0:T(8,128)(2,1)S(1)}, u32[]{:S(2)}, u32[]{:S(2)}) %collective-permute-start.2) | collective-permute-done | bytes 1048608 | tf_op jit(solution)/shard_map/ppermute | solution.py:14
  73.3 1.0 collective-permute-start.3
  74.3 0.7 fusion.40
  75.0 0.7 fusion.11
  76.4 19.4 %collective-permute-done.8 = f32[128,4096]{1,0:T(8,128)S(1)} collective-permute-done((f32[128,4096]{1,0:T(8,128)S(1)}, f32[128,4096]{1,0:T(8,128)S(1)}, u32[]{:S(2)}, u32[]{:S(2)}) %collective-permute-start.8) | collective-permute-done | bytes 2097184 | tf_op jit(solution)/shard_map/ppermute | solution.py:14
  96.0 1.1 collective-permute-start.9
  97.1 9.9 %collective-permute-done.3 = bf16[128,4096]{1,0:T(8,128)(2,1)S(1)} collective-permute-done((bf16[128,4096]{1,0:T(8,128)(2,1)S(1)}, bf16[128,4096]{1,0:T(8,128)(2,1)S(1)}, u32[]{:S(2)}, u32[]{:S(2)}) %collective-permute-start.3) | collective-permute-done | bytes 1048608 | tf_op jit(solution)/shard_map/ppermute | solution.py:14
  107.0 1.0 collective-permute-start.4
  108.7 0.7 fusion.12
  110.1 30.6 %collective-permute-done.4 = bf16[128,4096]{1,0:T(8,128)(2,1)S(1)} collective-permute-done((bf16[128,4096]{1,0:T(8,128)(2,1)S(1)}, bf16[128,4096]{1,0:T(8,128)(2,1)S(1)}, u32[]{:S(2)}, u32[]{:S(2)}) %collective-permute-start.4) | collective-permute-done | bytes 1048608 | tf_op jit(solution)/shard_map/ppermute | solution.py:14
  140.7 1.0 collective-permute-start.5
  142.2 0.7 fusion.13
  142.9 0.7 fusion.51
  143.9 2.9 collective-permute-start.10
  147.2 7.7 %collective-permute-done.5 = bf16[128,4096]{1,0:T(8,128)(2,1)S(1)} collective-permute-done((bf16[128,4096]{1,0:T(8,128)(2,1)S(1)}, bf16[128,4096]{1,0:T(8,128)(2,1)S(1)}, u32[]{:S(2)}, u32[]{:S(2)}) %collective-permute-start.5) | collective-permute-done | bytes 1048608 | tf_op jit(solution)/shard_map/ppermute | solution.py:14
  154.9 1.9 collective-permute-start.6
  156.8 0.7 fusion.14
  158.9 0.7 fusion.15
  159.6 2.6 fusion.49
  162.3 26.3 %collective-permute-done.6 = bf16[128,4096]{1,0:T(8,128)(2,1)S(1)} collective-permute-done((bf16[128,4096]{1,0:T(8,128)(2,1)S(1)}, bf16[128,4096]{1,0:T(8,128)(2,1)S(1)}, u32[]{:S(2)}, u32[]{:S(2)}) %collective-permute-start.6) | collective-permute-done | bytes 1048608 | tf_op jit(solution)/shard_map/ppermute | solution.py:14
  188.6 0.7 fusion.16
  189.4 2.7 fusion.48
  192.1 1.5 add.91
  193.6 1.9 collective-permute-start.11
  195.5 8.6 %fusion.39 = (f32[4096]{0:T(1024)}, bf16[256,4096]{1,0:T(8,128)(2,1)}) fusion(f32[256]{0:T(256)S(1)} %broadcast_add_fusion.1, f32[256,4096]{1,0:T(8,128)} %fusion.48, f32[256,4096]{1,0:T(8,128)} %fusion.49, f32[256,4096]{1,0:T(8,128)S(1)} %fusion.50, f32[256,4096]{1,0:T(8,128)S(1)} %fusion.51, f32[256,4096]{1,0:T(8,128)S(1)} %fusion.52, ...), kind=kOutput, calls=%fused_computation.64 | convolution fusion | flops 285208576 | bytes 30493696 | tf_op jit(solution)/shard_map/dot_general | solution.py:21
  204.2 1.3 fusion.45
  205.5 13.9 %collective-permute-done.11 = f32[128,4096]{1,0:T(8,128)} collective-permute-done((f32[128,4096]{1,0:T(8,128)}, f32[128,4096]{1,0:T(8,128)}, u32[]{:S(2)}, u32[]{:S(2)}) %collective-permute-start.11) | collective-permute-done | bytes 2097184 | tf_op jit(solution)/shard_map/ppermute | solution.py:14
  219.4 1.9 add.92
  221.2 2.9 collective-permute-start.12
  224.6 22.2 %collective-permute-done.12 = f32[128,4096]{1,0:T(8,128)S(1)} collective-permute-done((f32[128,4096]{1,0:T(8,128)S(1)}, f32[128,4096]{1,0:T(8,128)S(1)}, u32[]{:S(2)}, u32[]{:S(2)}) %collective-permute-start.12) | collective-permute-done | bytes 2097184 | tf_op jit(solution)/shard_map/ppermute | solution.py:14
  247.0 5.2 collective-permute-start.13
  252.7 19.8 %collective-permute-done.13 = f32[128,4096]{1,0:T(8,128)S(1)} collective-permute-done((f32[128,4096]{1,0:T(8,128)S(1)}, f32[128,4096]{1,0:T(8,128)S(1)}, u32[]{:S(2)}, u32[]{:S(2)}) %collective-permute-start.13) | collective-permute-done | bytes 2097184 | tf_op jit(solution)/shard_map/ppermute | solution.py:14
  272.8 7.9 %collective-permute-start.14 = (f32[128,4096]{1,0:T(8,128)S(1)}, f32[128,4096]{1,0:T(8,128)}, u32[]{:S(2)}, u32[]{:S(2)}) collective-permute-start(f32[128,4096]{1,0:T(8,128)S(1)} %add.94), channel_id=1, source_target_pairs={{25,0},{26,1},{27,2},{28,3},{29,4},{30,5},{31,6},{0,7},{1,8},{2,9}... | collective-permute-start | bytes 6291464 | tf_op jit(solution)/shard_map/ppermute | solution.py:14
  280.7 70.1 %collective-permute-done.14 = f32[128,4096]{1,0:T(8,128)} collective-permute-done((f32[128,4096]{1,0:T(8,128)S(1)}, f32[128,4096]{1,0:T(8,128)}, u32[]{:S(2)}, u32[]{:S(2)}) %collective-permute-start.14) | collective-permute-done | bytes 2097184 | tf_op jit(solution)/shard_map/ppermute | solution.py:14
  350.9 390.4 %all-gather.3.cloned.1.call-done = f32[1048576]{0:T(1024)} async-done(((f32[4096]{0:T(1024)}), f32[1048576]{0:T(1024)}) %all-gather.3.cloned.1.call-update) | async-done | bytes 4194320 | tf_op jit(solution)/shard_map/all_gather | solution.py:63
  741.2 5.0 reshape.17
  746.2 2.5 reduce_sum.39
  749.4 3.3 fusion.17
  (58 shorter events, 9.2 us)
Async XLA Ops:
  8.0 3.7 copy-start.10
  8.0 3.7 copy-start.1
  8.0 733.2 %all-gather.3.cloned.1.call-start = ((), (), s32[]{:S(2)}) async-start(), calls=%async_computation.1 | async-start | bytes 4210688 | tf_op jit(solution)/shard_map/all_gather | solution.py:63
  8.9 3.1 copy-start.11
  8.9 3.1 copy-start.2
  10.9 14.4 %collective-permute-start = (bf16[128,4096]{1,0:T(8,128)(2,1)S(1)}, bf16[128,4096]{1,0:T(8,128)(2,1)S(1)}, u32[]{:S(2)}, u32[]{:S(2)}) collective-permute-start(bf16[128,4096]{1,0:T(8,128)(2,1)S(1)} %fusion.18), channel_id=1, source_target_pairs={{1,0},{2,1},{3,2},{4,3},{5,4},{6,5},{7,6},{8,7},{9,8},{10,9},{11,1... | collective-permute-start | bytes 3145736 | tf_op jit(solution)/shard_map/ppermute | solution.py:14
  12.1 1.4 copy-start.3
  15.0 44.2 %collective-permute-start.7 = (f32[128,4096]{1,0:T(8,128)S(1)}, f32[128,4096]{1,0:T(8,128)S(1)}, u32[]{:S(2)}, u32[]{:S(2)}) collective-permute-start(f32[128,4096]{1,0:T(8,128)S(1)} %fusion.41), channel_id=1, source_target_pairs={{1,0},{2,1},{3,2},{4,3},{5,4},{6,5},{7,6},{8,7},{9,8},{10,9},{11,1... | collective-permute-start | bytes 6291464 | tf_op jit(solution)/shard_map/ppermute | solution.py:14
  25.3 33.7 %collective-permute-start.1 = (bf16[128,4096]{1,0:T(8,128)(2,1)S(1)}, bf16[128,4096]{1,0:T(8,128)(2,1)S(1)}, u32[]{:S(2)}, u32[]{:S(2)}) collective-permute-start(bf16[128,4096]{1,0:T(8,128)(2,1)S(1)} %collective-permute-done), channel_id=1, source_target_pairs={{1,0},{2,1},{3,2},{4,3},{5,4},{6,5},{7,6},{8,7},{9,8},{10,9},{11,1... | collective-permute-start | bytes 3145736 | tf_op jit(solution)/shard_map/ppermute | solution.py:14
  59.0 15.9 %copy-start.12 = (bf16[128,4096]{1,0:T(8,128)(2,1)}, bf16[128,4096]{1,0:T(8,128)(2,1)S(1)}, u32[]{:S(2)}) copy-start(bf16[128,4096]{1,0:T(8,128)(2,1)S(1)} %collective-permute-done.1) | copy-start | bytes 3145732
  59.0 14.2 %collective-permute-start.2 = (bf16[128,4096]{1,0:T(8,128)(2,1)S(1)}, bf16[128,4096]{1,0:T(8,128)(2,1)S(1)}, u32[]{:S(2)}, u32[]{:S(2)}) collective-permute-start(bf16[128,4096]{1,0:T(8,128)(2,1)S(1)} %collective-permute-done.1), channel_id=1, source_target_pairs={{1,0},{2,1},{3,2},{4,3},{5,4},{6,5},{7,6},{8,7},{9,8},{10,9},{11,1... | collective-permute-start | bytes 3145736 | tf_op jit(solution)/shard_map/ppermute | solution.py:14
  59.7 36.1 %collective-permute-start.8 = (f32[128,4096]{1,0:T(8,128)S(1)}, f32[128,4096]{1,0:T(8,128)S(1)}, u32[]{:S(2)}, u32[]{:S(2)}) collective-permute-start(f32[128,4096]{1,0:T(8,128)S(1)} %convolution_add_fusion.2), channel_id=1, source_target_pairs={{1,0},{2,1},{3,2},{4,3},{5,4},{6,5},{7,6},{8,7},{9,8},{10,9},{11,1... | collective-permute-start | bytes 6291464 | tf_op jit(solution)/shard_map/ppermute | solution.py:14
  73.3 33.7 %collective-permute-start.3 = (bf16[128,4096]{1,0:T(8,128)(2,1)S(1)}, bf16[128,4096]{1,0:T(8,128)(2,1)S(1)}, u32[]{:S(2)}, u32[]{:S(2)}) collective-permute-start(bf16[128,4096]{1,0:T(8,128)(2,1)S(1)} %collective-permute-done.2), channel_id=1, source_target_pairs={{1,0},{2,1},{3,2},{4,3},{5,4},{6,5},{7,6},{8,7},{9,8},{10,9},{11,1... | collective-permute-start | bytes 3145736 | tf_op jit(solution)/shard_map/ppermute | solution.py:14
  75.7 0.6 copy-start.9
  96.0 47.6 %collective-permute-start.9 = (f32[128,4096]{1,0:T(8,128)S(1)}, f32[128,4096]{1,0:T(8,128)S(1)}, u32[]{:S(2)}, u32[]{:S(2)}) collective-permute-start(f32[128,4096]{1,0:T(8,128)S(1)} %add.89), channel_id=1, source_target_pairs={{1,0},{2,1},{3,2},{4,3},{5,4},{6,5},{7,6},{8,7},{9,8},{10,9},{11,1... | collective-permute-start | bytes 6291464 | tf_op jit(solution)/shard_map/ppermute | solution.py:14
  107.0 33.7 %collective-permute-start.4 = (bf16[128,4096]{1,0:T(8,128)(2,1)S(1)}, bf16[128,4096]{1,0:T(8,128)(2,1)S(1)}, u32[]{:S(2)}, u32[]{:S(2)}) collective-permute-start(bf16[128,4096]{1,0:T(8,128)(2,1)S(1)} %collective-permute-done.3), channel_id=1, source_target_pairs={{1,0},{2,1},{3,2},{4,3},{5,4},{6,5},{7,6},{8,7},{9,8},{10,9},{11,1... | collective-permute-start | bytes 3145736 | tf_op jit(solution)/shard_map/ppermute | solution.py:14
  140.7 14.2 %collective-permute-start.5 = (bf16[128,4096]{1,0:T(8,128)(2,1)S(1)}, bf16[128,4096]{1,0:T(8,128)(2,1)S(1)}, u32[]{:S(2)}, u32[]{:S(2)}) collective-permute-start(bf16[128,4096]{1,0:T(8,128)(2,1)S(1)} %collective-permute-done.4), channel_id=1, source_target_pairs={{1,0},{2,1},{3,2},{4,3},{5,4},{6,5},{7,6},{8,7},{9,8},{10,9},{11,1... | collective-permute-start | bytes 3145736 | tf_op jit(solution)/shard_map/ppermute | solution.py:14
  143.9 48.2 %collective-permute-start.10 = (f32[128,4096]{1,0:T(8,128)S(1)}, f32[128,4096]{1,0:T(8,128)S(1)}, u32[]{:S(2)}, u32[]{:S(2)}) collective-permute-start(f32[128,4096]{1,0:T(8,128)S(1)} %add.90), channel_id=1, source_target_pairs={{1,0},{2,1},{3,2},{4,3},{5,4},{6,5},{7,6},{8,7},{9,8},{10,9},{11,1... | collective-permute-start | bytes 6291464 | tf_op jit(solution)/shard_map/ppermute | solution.py:14
  154.9 33.7 %collective-permute-start.6 = (bf16[128,4096]{1,0:T(8,128)(2,1)S(1)}, bf16[128,4096]{1,0:T(8,128)(2,1)S(1)}, u32[]{:S(2)}, u32[]{:S(2)}) collective-permute-start(bf16[128,4096]{1,0:T(8,128)(2,1)S(1)} %collective-permute-done.5), channel_id=1, source_target_pairs={{1,0},{2,1},{3,2},{4,3},{5,4},{6,5},{7,6},{8,7},{9,8},{10,9},{11,1... | collective-permute-start | bytes 3145736 | tf_op jit(solution)/shard_map/ppermute | solution.py:14
  157.6 0.6 copy-start.8
  159.6 2.7 copy-start.6
  189.3 2.7 copy-start.4
  193.6 25.8 %collective-permute-start.11 = (f32[128,4096]{1,0:T(8,128)}, f32[128,4096]{1,0:T(8,128)}, u32[]{:S(2)}, u32[]{:S(2)}) collective-permute-start(f32[128,4096]{1,0:T(8,128)} %add.91), channel_id=1, source_target_pairs={{1,0},{2,1},{3,2},{4,3},{5,4},{6,5},{7,6},{8,7},{9,8},{10,9},{11,1... | collective-permute-start | bytes 6291464 | tf_op jit(solution)/shard_map/ppermute | solution.py:14
  204.1 545.3 %all-reduce.2.cloned.1.call-start = ((), (), s32[]{:S(2)}) async-start(), calls=%async_computation | async-start | bytes 4194304 | tf_op jit(solution)/shard_map/psum | solution.py:62
  205.5 18.6 %copy-start.7 = (bf16[256,128]{1,0:T(8,128)(2,1)S(1)}, bf16[256,128]{1,0:T(8,128)(2,1)}, u32[]{:S(2)}) copy-start(bf16[256,128]{1,0:T(8,128)(2,1)} %copy-done.6) | copy-start | bytes 196612
  221.2 25.5 %collective-permute-start.12 = (f32[128,4096]{1,0:T(8,128)S(1)}, f32[128,4096]{1,0:T(8,128)S(1)}, u32[]{:S(2)}, u32[]{:S(2)}) collective-permute-start(f32[128,4096]{1,0:T(8,128)S(1)} %add.92), channel_id=1, source_target_pairs={{1,0},{2,1},{3,2},{4,3},{5,4},{6,5},{7,6},{8,7},{9,8},{10,9},{11,1... | collective-permute-start | bytes 6291464 | tf_op jit(solution)/shard_map/ppermute | solution.py:14
  224.6 27.7 %copy-start.5 = (bf16[256,128]{1,0:T(8,128)(2,1)S(1)}, bf16[256,128]{1,0:T(8,128)(2,1)}, u32[]{:S(2)}) copy-start(bf16[256,128]{1,0:T(8,128)(2,1)} %copy-done.4) | copy-start | bytes 196612
  247.0 25.5 %collective-permute-start.13 = (f32[128,4096]{1,0:T(8,128)S(1)}, f32[128,4096]{1,0:T(8,128)S(1)}, u32[]{:S(2)}, u32[]{:S(2)}) collective-permute-start(f32[128,4096]{1,0:T(8,128)S(1)} %add.93), channel_id=1, source_target_pairs={{1,0},{2,1},{3,2},{4,3},{5,4},{6,5},{7,6},{8,7},{9,8},{10,9},{11,1... | collective-permute-start | bytes 6291464 | tf_op jit(solution)/shard_map/ppermute | solution.py:14
  272.8 78.0 %collective-permute-start.14 = (f32[128,4096]{1,0:T(8,128)S(1)}, f32[128,4096]{1,0:T(8,128)}, u32[]{:S(2)}, u32[]{:S(2)}) collective-permute-start(f32[128,4096]{1,0:T(8,128)S(1)} %add.94), channel_id=1, source_target_pairs={{25,0},{26,1},{27,2},{28,3},{29,4},{30,5},{31,6},{0,7},{1,8},{2,9}... | collective-permute-start | bytes 6291464 | tf_op jit(solution)/shard_map/ppermute | solution.py:14
  746.2 3.2 copy-start
Sparse Core Ops, SparseCore 0:
  204.2 536.9 all-gather.2
Sparse Core Ops, SparseCore 1:
  351.0 132.9 all-reduce.1
